TPU v7x, 128 devices: a whole 4x4x4 slice. The times are simulated.
128 devices in a mesh: bx: 4 (over y), by: 4 (over x), bz: 8 (over z, core).
Axes of the slice: x: 4, y: 4, z: 4, core: 2. Of those that a mesh axis runs over, the one named last changes fastest.
Arguments:
- position: float32 [3, 128, 128, 2048], P(None, 'bx', 'by', 'bz'), may hold values from -2 to 2
- velocity: float32 [3, 128, 128, 2048], P(None, 'bx', 'by', 'bz'), may hold values from -3 to 3
- density: float32 [128, 128, 2048], P('bx', 'by', 'bz'), may hold values from 0.5 to 2
- energy: float32 [128, 128, 2048], P('bx', 'by', 'bz'), may hold values from 0.1 to 10
- pinned: int32 [128, 128, 2048], P('bx', 'by', 'bz'), may hold values 0 or 1
Outputs:
- velocity_new: float32 [3, 128, 128, 2048], P(None, 'bx', 'by', 'bz')
- accel: float32 [3, 128, 128, 2048], P(None, 'bx', 'by', 'bz')
- relaxed: float32 [3, 128, 128, 2048], P(None, 'bx', 'by', 'bz')
- density_new: float32 [128, 128, 2048], P('bx', 'by', 'bz')
- energy_new: float32 [128, 128, 2048], P('bx', 'by', 'bz')
All inputs are finite; a program needn't handle non-finite values. No bound on the sum of `pinned` on one device may be relied on, other than what follows from the above.
Results may differ from a plain program's by a relative error of at most 0.0003.
Values sent between devices are 32-bit elements; how exact they have to be, the bound alone decides.
A program may use at most 128 MiB of HBM per device.

v0:
```python
import jax
import jax.numpy as jnp
from jax import lax
from jax.sharding import PartitionSpec as P

CG_ITERS = 2
SWEEPS = 3
TIME_STEP = 0.6
RELAX_RATE = 0.8
CONSISTENT = 0.2


def from_behind(x, axis, by):
    length = lax.axis_size(axis)
    pairs = [(i, i + by) for i in range(length) if 0 <= i + by < length]
    return lax.ppermute(x, axis, pairs)


def padded(block, sides, width):
    for axis, dim in sides:
        count = lax.axis_size(axis)
        forward = [(i, i + 1) for i in range(count - 1)]
        backward = [(target, source) for source, target in forward]
        low = lax.ppermute(
            lax.slice_in_dim(block, block.shape[dim] - width, None, axis=dim), axis, forward
        )
        high = lax.ppermute(lax.slice_in_dim(block, 0, width, axis=dim), axis, backward)
        block = jnp.concatenate([low, block, high], axis=dim)
    return block


def shift_triple(along_dim, along, first, second):
    offsets = [0, 0, 0]
    offsets[along_dim] = along
    others = [d for d in range(3) if d != along_dim]
    offsets[others[0]] = first
    offsets[others[1]] = second
    return offsets


def select_at(extended, offsets):
    sizes = extended.shape[-3:]
    return extended[
        ...,
        1 + offsets[0] : sizes[0] - 1 + offsets[0],
        1 + offsets[1] : sizes[1] - 1 + offsets[1],
        1 + offsets[2] : sizes[2] - 1 + offsets[2],
    ]


def corner_force(pressure_ext):
    parts = []
    for along_dim in range(3):
        summed = 0.0
        for first in (0, -1):
            for second in (0, -1):
                summed = (
                    summed
                    + select_at(pressure_ext, shift_triple(along_dim, -1, first, second))
                    - select_at(pressure_ext, shift_triple(along_dim, 0, first, second))
                )
        parts.append(0.25 * summed)
    return jnp.stack(parts)


def node_mass(density_ext):
    summed = 0.0
    for first in (0, -1):
        for second in (0, -1):
            for third in (0, -1):
                summed = summed + select_at(density_ext, [first, second, third])
    return 0.125 * summed


def neighbours(extended):
    summed = 0.0
    for along_dim in range(3):
        for along in (-1, 1):
            summed = summed + select_at(extended, shift_triple(along_dim, along, 0, 0))
    return summed


def divergence(vel_ext):
    summed = 0.0
    for along_dim in range(3):
        for first in (0, 1):
            for second in (0, 1):
                summed = (
                    summed
                    + select_at(vel_ext[along_dim], shift_triple(along_dim, 1, first, second))
                    - select_at(vel_ext[along_dim], shift_triple(along_dim, 0, first, second))
                )
    return 0.25 * summed


def face_flux(packed, along_dim, along):
    speed = 0.0
    for first in (0, 1):
        for second in (0, 1):
            speed = speed + select_at(
                packed[along_dim], shift_triple(along_dim, along, first, second)
            )
    speed = 0.25 * speed
    upper = select_at(packed[3:5], shift_triple(along_dim, along, 0, 0))
    lower = select_at(packed[3:5], shift_triple(along_dim, along - 1, 0, 0))
    return speed * jnp.where(speed > 0, upper, lower)


def remap_cells(packed):
    result = select_at(packed[3:5], [0, 0, 0])
    for along_dim in range(3):
        result = result + face_flux(packed, along_dim, 1) - face_flux(packed, along_dim, 0)
    return result


def inner(first, second):
    return jnp.sum(first * second, axis=(1, 2, 3), keepdims=True)


def lower_cells(values):
    got = from_behind(values[..., -1:, :, :], "bx", 1)
    widened = jnp.concatenate([got, values], axis=-3)
    got = from_behind(widened[..., :, -1:, :], "by", 1)
    widened = jnp.concatenate([got, widened], axis=-2)
    got = from_behind(widened[..., :, :, -1:], "bz", 1)
    widened = jnp.concatenate([got, widened], axis=-1)
    return jnp.pad(widened, [(0, 0)] * (values.ndim - 3) + [(0, 1)] * 3)


def upper_nodes(values):
    got = from_behind(values[..., :1, :, :], "bx", -1)
    widened = jnp.concatenate([values, got], axis=-3)
    got = from_behind(widened[..., :, :1, :], "by", -1)
    widened = jnp.concatenate([widened, got], axis=-2)
    got = from_behind(widened[..., :, :, :1], "bz", -1)
    widened = jnp.concatenate([widened, got], axis=-1)
    return jnp.pad(widened, [(0, 0)] * (values.ndim - 3) + [(1, 0)] * 3)


def mass_apply(vector, masses):
    extended = padded(vector, (("bx", 1), ("by", 2), ("bz", 3)), 1)
    return masses * vector + CONSISTENT * (6.0 * vector + neighbours(extended))


def squares(residual):
    return lax.psum(inner(residual, residual), ("bx", "by", "bz"))


def one_sweep(relaxed, free):
    extended = padded(relaxed, (("bx", 1), ("by", 2), ("bz", 3)), 1)
    return relaxed + RELAX_RATE * free * (neighbours(extended) / 6.0 - relaxed)


def on_device(position, velocity, density, energy, pinned):
    cells = lower_cells(jnp.stack([density, energy]))
    force = corner_force(0.4 * cells[0] * cells[1])
    masses = node_mass(cells[0])
    solution = jnp.zeros_like(force)
    residual = force
    direction = force
    norm_now = squares(residual)
    for step_index in range(CG_ITERS):
        image = mass_apply(direction, masses)
        alpha = norm_now / lax.psum(inner(direction, image), ("bx", "by", "bz"))
        solution = solution + alpha * direction
        residual = residual - alpha * image
        norm_next = squares(residual)
        direction = residual + norm_next / norm_now * direction
        norm_now = norm_next
    velocity_new = velocity + TIME_STEP * solution
    vel_ext = upper_nodes(velocity_new)
    spread = divergence(vel_ext)
    pressure = 0.4 * density * energy
    energy_lag = energy - TIME_STEP * pressure * spread / density
    moved = position + TIME_STEP * velocity_new
    free = 1.0 - pinned.astype(jnp.float32)
    relaxed = moved
    for step_index in range(SWEEPS):
        relaxed = one_sweep(relaxed, free)
    packed = padded(
        jnp.concatenate([relaxed - moved, density[None], (density * energy_lag)[None]]),
        (("bx", 1), ("by", 2), ("bz", 3)),
        1,
    )
    remapped = remap_cells(packed)
    return (velocity_new, solution, relaxed, remapped[0], remapped[1])


def solution(mesh):
    in_specs = (
        P(None, "bx", "by", "bz"),
        P(None, "bx", "by", "bz"),
        P("bx", "by", "bz"),
        P("bx", "by", "bz"),
        P("bx", "by", "bz"),
    )
    out_specs = (
        P(None, "bx", "by", "bz"),
        P(None, "bx", "by", "bz"),
        P(None, "bx", "by", "bz"),
        P("bx", "by", "bz"),
        P("bx", "by", "bz"),
    )
    return jax.shard_map(
        on_device, mesh=mesh, in_specs=in_specs, out_specs=out_specs, check_vma=False
    )
```

profile of v0, /device:TPU:1, one launch (start us, length us, event | category | flops | bytes accessed | tf_op | source)
XLA Modules:
  0.0 638.1 jit_solution(13406718772434215634)
XLA Ops:
  1.6 4.0 collective-permute-start
  8.0 3.1 collective-permute-start.1
  14.1 5.8 collective-permute-start.2
  22.3 3.6 select_maximum_fusion.3
  29.0 4.0 collective-permute-start.3
  34.6 3.7 collective-permute-done.4
  38.5 4.0 collective-permute-start.5
  45.3 4.1 collective-permute-done.6
  52.9 3.0 copy.64
  55.9 3.0 copy.66
  61.2 5.9 collective-permute-start.7
  67.1 7.7 %fusion.120 = f32[32,32,256]{2,1,0:T(8,128)} fusion(f32[34,34,258]{2,1,0:T(8,128)} %slice_bitcast_fusion.7), kind=kLoop, calls=%fused_computation.316 | loop fusion | flops 2097152 | bytes 9437184 | tf_op jit(solution)/shard_map/mul | solution.py:72
  74.8 2.9 copy.65
  77.8 2.9 copy.67
  80.7 16.0 %multiply_reduce_fusion.1 = (f32[3]{0:T(128)}, f32[3]{0:T(128)}, f32[3,32,32,256]{3,2,1,0:T(8,128)}) fusion(f32[1,32,32,256]{3,2,1,0:T(8,128)} %copy-done.4, f32[1,32,32,256]{3,2,1,0:T(8,128)S(1)} %multiply_bitcast_fusion.1, f32[1,32,32,256]{3,2,1,0:T(8,128)S(1)} %get-tuple-element.82, f32[3,34,34,1]{3,2,1,0:T(8,128)} %copy.67, ...), kind=kLoop, calls=%fused_computation.195 | loop fusion | flops 36175864 | bytes 7773304 | tf_op jit(solution)/shard_map/reduce_sum | solution.py:117
  96.7 64.6 %all-reduce.2 = (f32[3,1,1,1]{0,3,2,1:T(1,128)S(1)}, f32[3,1,1,1]{0,3,2,1:T(1,128)S(1)}) all-reduce(f32[3,1,1,1]{0,3,2,1:T(1,128)} %bitcast.58, f32[3,1,1,1]{0,3,2,1:T(1,128)} %bitcast.57), channel_id=1, replica_groups=mesh['bx'=4,'by'=4,'bz'=8] {'bx','by','bz'}, use_global_device_ids=true, to_apply=%region_1.2 | all-reduce | flops 6 | bytes 48 | tf_op jit(solution)/shard_map/psum | solution.py:146
  164.2 63.1 %psum.30 = f32[3,1,1,1]{0,3,2,1:T(1,128)S(1)} all-reduce(f32[3,1,1,1]{0,3,2,1:T(1,128)S(1)} %bitcast.60), channel_id=1, replica_groups=mesh['bx'=4,'by'=4,'bz'=8] {'bx','by','bz'}, use_global_device_ids=true, to_apply=%region_5.6 | all-reduce | flops 3 | bytes 24 | tf_op jit(solution)/shard_map/psum | solution.py:146
  227.3 3.1 multiply_add_fusion.3
  234.4 3.7 collective-permute-done.10
  241.7 3.8 collective-permute-done.12
  248.8 3.0 copy.68
  251.8 5.8 collective-permute-start.13
  257.6 3.0 copy.70
  262.7 2.9 copy.69
  266.4 2.9 copy.71
  269.3 15.8 %fusion.67 = f32[3]{0:T(128)} fusion(f32[3,32,32,256]{3,2,1,0:T(8,128)} %copy-done.5, f32[3,34,34,1]{3,2,1,0:T(8,128)} %copy.71, f32[3,34,1,256]{3,2,1,0:T(1,128)S(1)} %collective-permute-done.12, f32[3,34,1,256]{3,2,1,0:T(1,128)S(1)} %collective-permute-done.11, f32[3,1,32,256]{3,2,1,0:T(8,128)S(1)} %collective-permute-done.10, ...), kind=kLoop, calls=%fused_computation.147 | loop fusion | flops 23592956 | bytes 4627564 | tf_op jit(solution)/shard_map/reduce_sum | solution.py:117
  285.1 63.9 %psum.31 = f32[3,1,1,1]{0,3,2,1:T(1,128)S(1)} all-reduce(f32[3,1,1,1]{0,3,2,1:T(1,128)} %bitcast.59), channel_id=1, replica_groups=mesh['bx'=4,'by'=4,'bz'=8] {'bx','by','bz'}, use_global_device_ids=true, to_apply=%region_7.8 | all-reduce | flops 3 | bytes 24 | tf_op jit(solution)/shard_map/psum | solution.py:164
  349.7 6.8 %multiply_add_fusion = (f32[3,32,32,256]{3,2,1,0:T(8,128)S(1)}, f32[3,32,32,256]{3,2,1,0:T(8,128)}, f32[3,32,32,256]{3,2,1,0:T(8,128)}) fusion(f32[3,32,32,256]{3,2,1,0:T(8,128)} %param.5, f32[3,32,32,256]{3,2,1,0:T(8,128)} %param.6, f32[3]{0:T(128)S(1)} %divide_bitcast_fusion, f32[1,32,32,256]{3,2,1,0:T(8,128)} %copy-done.4, ...), kind=kLoop, calls=%fused_computation.189 | loop fusion | flops 10223616 | bytes 22020132 | tf_op jit(solution)/shard_map/add | solution.py:175
  360.3 3.7 collective-permute-done.16
  365.6 4.0 collective-permute-start.17
  374.2 3.1 copy.78
  378.9 5.4 collective-permute-start.20
  392.2 14.2 %fusion.57 = f32[3,32,32,256]{3,2,1,0:T(8,128)S(1)} fusion(f32[3,32,32,256]{3,2,1,0:T(8,128)} %copy-done.3, f32[3,34,34,1]{3,2,1,0:T(8,128)} %copy.81, f32[3,34,1,256]{3,2,1,0:T(1,128)S(1)} %copy.75, f32[3,34,1,256]{3,2,1,0:T(1,128)S(1)} %copy.73, f32[3,1,32,256]{3,2,1,0:T(8,128)S(1)} %collective-permute-done.16, ...), kind=kLoop, calls=%fused_computation.119 | loop fusion | flops 21233664 | bytes 7773280 | tf_op jit(solution)/shard_map/add | solution.py:151
  416.1 4.7 collective-permute-start.23
  422.2 4.3 collective-permute-done.34
  435.3 5.6 collective-permute-start.26
  440.9 3.8 collective-permute-start.25
  444.7 2.9 pad_maximum_fusion.113
  452.0 3.6 collective-permute-done.35
  462.1 14.5 %fusion.48 = f32[3,32,32,256]{3,2,1,0:T(8,128)S(1)} fusion(f32[3,32,32,256]{3,2,1,0:T(8,128)} %copy-done.6, f32[3,34,34,1]{3,2,1,0:T(8,128)} %copy.91, f32[3,34,1,256]{3,2,1,0:T(1,128)S(1)} %copy.85, f32[3,34,1,256]{3,2,1,0:T(1,128)S(1)} %copy.83, f32[3,1,32,256]{3,2,1,0:T(8,128)S(1)} %collective-permute-done.22, ...), kind=kLoop, calls=%fused_computation.92 | loop fusion | flops 21233664 | bytes 7773280 | tf_op jit(solution)/shard_map/add | solution.py:151
  476.6 3.2 collective-permute-start.27
  481.2 4.7 select_maximum_fusion
  487.4 4.7 collective-permute-start.29
  498.2 3.1 copy.98
  501.3 3.1 copy.100
  506.4 3.6 collective-permute-start.31
  510.0 20.4 %fusion.119 = f32[1,32,32,256]{3,2,1,0:T(8,128)} fusion(f32[32,32,256]{2,1,0:T(8,128)S(1)} %copy-done, f32[32,32,256]{2,1,0:T(8,128)} %param.8, f32[34,34,258]{2,1,0:T(8,128)} %get-tuple-element.39, f32[34,34,258]{2,1,0:T(8,128)} %get-tuple-element.38, f32[34,34,258]{2,1,0:T(8,128)S(1)} %get-tuple-element.37), kind=kLoop, calls=%fused_computation.292 | loop fusion | flops 8126464 | bytes 28311552 | tf_op jit(solution)/shard_map/broadcast_in_dim | solution.py:181
  530.4 3.0 copy.99
  533.4 3.0 copy.101
  536.4 16.5 %fusion.127 = (f32[3,32,32,256]{3,2,1,0:T(8,128)S(1)}, f32[3,32,32,256]{3,2,1,0:T(8,128)}) fusion(f32[3,32,32,256]{3,2,1,0:T(8,128)} %copy-done.3, f32[3,32,32,256]{3,2,1,0:T(8,128)} %copy-done.7, f32[3,34,34,1]{3,2,1,0:T(8,128)} %copy.101, f32[3,34,1,256]{3,2,1,0:T(1,128)S(1)} %copy.95, f32[3,1,32,256]{3,2,1,0:T(8,128)S(1)} %collective-permute-done.28, ...), kind=kLoop, calls=%fused_computation.365 | loop fusion | flops 22020096 | bytes 14064736 | tf_op jit(solution)/shard_map/sub | solution.py:181
  552.9 4.0 collective-permute-start.36
  560.8 4.1 collective-permute-done.37
  565.2 3.4 collective-permute-start.38
  571.8 3.8 collective-permute-done.39
  577.2 3.9 fusion.130
  581.1 3.5 copy.107
  584.5 3.6 collective-permute-start.41
  588.1 3.5 copy.106
  593.7 3.5 copy.109
  597.2 3.5 copy.108
  600.7 16.1 %pad_maximum_fusion = f32[5,34,34,258]{3,2,1,0:T(8,128)S(1)} fusion(f32[5,34,34,1]{3,2,1,0:T(8,128)} %copy.109, f32[5,34,1,256]{3,2,1,0:T(1,128)} %copy-done.19, f32[5,1,32,256]{3,2,1,0:T(8,128)S(1)} %collective-permute-done.37, f32[1,32,32,256]{3,2,1,0:T(8,128)} %fusion.119, f32[1,32,32,256]{3,2,1,0:T(8,128)} %bitcast.46, ...), kind=kLoop, calls=%fused_computation | loop fusion | flops 11929920 | bytes 11929920 | tf_op jit(solution)/shard_map/concatenate | solution.py:28
  617.2 3.7 broadcast_compare_fusion.5
  621.0 6.0 broadcast_compare_fusion.1
  627.1 9.3 %fusion.84 = f32[2,32,32,256]{3,2,1,0:T(8,128)S(1)} fusion(f32[3,32,32,256]{3,2,1,0:T(8,128)S(1)} %get-tuple-element.26, f32[1,32,32,256]{3,2,1,0:T(8,128)S(1)} %bitcast.52, f32[5,34,34,1]{3,2,1,0:T(8,128)S(1)} %copy-done.13, f32[5,34,1,256]{3,2,1,0:T(1,128)S(1)} %copy-done.20, f32[5,34,1,256]{3,2,1,0:T(1,128)S(1)} %copy-done.18, ...), kind=kLoop, calls=%fused_computation.206 | loop fusion | flops 25690112 | bytes 15926432 | tf_op jit(solution)/shard_map/sub | solution.py:112
  (173 shorter events, 113.0 us)
Async XLA Ops:
  0.6 12.5 %copy-start.14 = (f32[32,32,256]{2,1,0:T(8,128)S(1)}, f32[32,32,256]{2,1,0:T(8,128)}, u32[]{:S(2)}) copy-start(f32[32,32,256]{2,1,0:T(8,128)} %param.8) | copy-start | bytes 3145732
  0.6 12.5 %copy-start = (f32[32,32,256]{2,1,0:T(8,128)S(1)}, f32[32,32,256]{2,1,0:T(8,128)}, u32[]{:S(2)}) copy-start(f32[32,32,256]{2,1,0:T(8,128)} %param.7) | copy-start | bytes 3145732
  1.6 5.3 collective-permute-start
  8.0 4.5 collective-permute-start.1
  14.1 6.8 %collective-permute-start.2 = (f32[2,33,33,1]{2,0,3,1:T(2,128)S(1)}, f32[2,33,33,1]{2,0,3,1:T(2,128)}, u32[]{:S(2)}, u32[]{:S(2)}) collective-permute-start(f32[2,33,33,1]{2,0,3,1:T(2,128)S(1)} %copy.62), channel_id=1, source_target_pairs={{0,1},{1,2},{2,3},{3,4},{4,5},{5,6},{6,7},{8,9},{9,10},{10,11},{11... | collective-permute-start | bytes 26144 | tf_op jit(solution)/shard_map/ppermute | solution.py:16
  28.7 21.6 %copy-start.4 = (f32[1,32,32,256]{3,2,1,0:T(8,128)}, f32[1,32,32,256]{3,2,1,0:T(8,128)S(1)}, u32[]{:S(2)}) copy-start(f32[1,32,32,256]{3,2,1,0:T(8,128)S(1)} %get-tuple-element.83) | copy-start | bytes 3145732
  29.0 5.6 collective-permute-start.3
  33.0 5.4 collective-permute-start.4
  38.5 6.8 %collective-permute-start.5 = (f32[3,34,1,256]{3,2,1,0:T(1,128)S(1)}, f32[3,34,1,256]{3,2,1,0:T(1,128)S(1)}, u32[]{:S(2)}, u32[]{:S(2)}) collective-permute-start(f32[3,34,1,256]{3,2,1,0:T(1,128)S(1)} %get-tuple-element.62), channel_id=1, source_target_pairs={{0,8},{8,16},{16,24},{1,9},{9,17},{17,25},{2,10},{10,18},{18,26},{... | collective-permute-start | bytes 313352 | tf_op jit(solution)/shard_map/ppermute | solution.py:24
  42.5 6.8 %collective-permute-start.6 = (f32[3,34,1,256]{3,2,1,0:T(1,128)S(1)}, f32[3,34,1,256]{3,2,1,0:T(1,128)S(1)}, u32[]{:S(2)}, u32[]{:S(2)}) collective-permute-start(f32[3,34,1,256]{3,2,1,0:T(1,128)S(1)} %get-tuple-element.63), channel_id=1, source_target_pairs={{8,0},{16,8},{24,16},{9,1},{17,9},{25,17},{10,2},{18,10},{26,18},{... | collective-permute-start | bytes 313352 | tf_op jit(solution)/shard_map/ppermute | solution.py:27
  58.9 18.8 %collective-permute-start.8 = (f32[3,34,34,1]{2,3,1,0:T(1,128)}, f32[3,34,34,1]{2,3,1,0:T(1,128)}, u32[]{:S(2)}, u32[]{:S(2)}) collective-permute-start(f32[3,34,34,1]{2,3,1,0:T(1,128)} %copy.66), channel_id=1, source_target_pairs={{1,0},{2,1},{3,2},{4,3},{5,4},{6,5},{7,6},{9,8},{10,9},{11,10},{12... | collective-permute-start | bytes 41624 | tf_op jit(solution)/shard_map/ppermute | solution.py:27
  61.2 13.6 %collective-permute-start.7 = (f32[3,34,34,1]{2,3,1,0:T(1,128)}, f32[3,34,34,1]{2,3,1,0:T(1,128)}, u32[]{:S(2)}, u32[]{:S(2)}) collective-permute-start(f32[3,34,34,1]{2,3,1,0:T(1,128)} %copy.64), channel_id=1, source_target_pairs={{0,1},{1,2},{2,3},{3,4},{4,5},{5,6},{6,7},{8,9},{9,10},{10,11},{11... | collective-permute-start | bytes 41624 | tf_op jit(solution)/shard_map/ppermute | solution.py:24
  161.3 66.0 %copy-start.22 = (f32[3]{0:T(128)}, f32[3]{0:T(128)S(1)}, u32[]{:S(2)}) copy-start(f32[3]{0:T(128)S(1)} %divide_bitcast_fusion.2) | copy-start | bytes 40
  227.2 3.1 copy-start.23
  230.4 15.8 %copy-start.5 = (f32[3,32,32,256]{3,2,1,0:T(8,128)}, f32[3,32,32,256]{3,2,1,0:T(8,128)S(1)}, u32[]{:S(2)}) copy-start(f32[3,32,32,256]{3,2,1,0:T(8,128)S(1)} %multiply_add_fusion.3) | copy-start | bytes 9437188
  230.4 4.0 collective-permute-start.9
  232.8 5.4 collective-permute-start.10
  238.3 3.4 collective-permute-start.11
  240.0 5.4 collective-permute-start.12
  251.8 10.9 %collective-permute-start.13 = (f32[3,34,34,1]{2,3,1,0:T(1,128)}, f32[3,34,34,1]{2,3,1,0:T(1,128)}, u32[]{:S(2)}, u32[]{:S(2)}) collective-permute-start(f32[3,34,34,1]{2,3,1,0:T(1,128)} %copy.68), channel_id=1, source_target_pairs={{0,1},{1,2},{2,3},{3,4},{4,5},{5,6},{6,7},{8,9},{9,10},{10,11},{11... | collective-permute-start | bytes 41624 | tf_op jit(solution)/shard_map/ppermute | solution.py:24
  260.6 5.7 collective-permute-start.14
  356.5 17.7 %copy-start.3 = (f32[3,32,32,256]{3,2,1,0:T(8,128)}, f32[3,32,32,256]{3,2,1,0:T(8,128)S(1)}, u32[]{:S(2)}) copy-start(f32[3,32,32,256]{3,2,1,0:T(8,128)S(1)} %get-tuple-element.28) | copy-start | bytes 9437188
  356.5 3.8 collective-permute-start.15
  358.7 5.4 collective-permute-start.16
  364.2 5.6 collective-permute-start.18
  365.6 5.8 collective-permute-start.17
  378.9 11.1 %collective-permute-start.20 = (f32[3,34,34,1]{2,1,3,0:T(8,128)}, f32[3,34,34,1]{2,1,3,0:T(8,128)S(1)}, u32[]{:S(2)}, u32[]{:S(2)}) collective-permute-start(f32[3,34,34,1]{2,1,3,0:T(8,128)} %copy.80), channel_id=1, source_target_pairs={{1,0},{2,1},{3,2},{4,3},{5,4},{6,5},{7,6},{9,8},{10,9},{11,10},{12... | collective-permute-start | bytes 41624 | tf_op jit(solution)/shard_map/ppermute | solution.py:27
  384.3 3.5 collective-permute-start.19
  387.8 74.3 %copy-start.15 = (f32[32,32,256]{2,1,0:T(8,128)}, f32[32,32,256]{2,1,0:T(8,128)S(1)}, u32[]{:S(2)}) copy-start(f32[32,32,256]{2,1,0:T(8,128)S(1)} %subtract_multiply_fusion) | copy-start | bytes 3145732
  392.2 18.3 %copy-start.8 = (f32[3,32,32,256]{3,2,1,0:T(8,128)S(1)}, f32[3,32,32,256]{3,2,1,0:T(8,128)}, u32[]{:S(2)}) copy-start(f32[3,32,32,256]{3,2,1,0:T(8,128)} %get-tuple-element.29) | copy-start | bytes 9437188
  406.4 20.5 %copy-start.6 = (f32[3,32,32,256]{3,2,1,0:T(8,128)}, f32[3,32,32,256]{3,2,1,0:T(8,128)S(1)}, u32[]{:S(2)}) copy-start(f32[3,32,32,256]{3,2,1,0:T(8,128)S(1)} %fusion.57) | copy-start | bytes 9437188
  406.4 5.5 collective-permute-start.21
  409.2 5.4 collective-permute-start.22
  410.6 10.2 %collective-permute-start.33 = (f32[3,1,32,256]{3,2,1,0:T(8,128)S(1)}, f32[3,1,32,256]{3,2,1,0:T(8,128)S(1)}, u32[]{:S(2)}, u32[]{:S(2)}) collective-permute-start(f32[3,1,32,256]{3,2,1,0:T(8,128)S(1)} %slice.782), channel_id=1, source_target_pairs={{32,0},{64,32},{96,64},{33,1},{65,33},{97,65},{34,2},{66,34},{98,6... | collective-permute-start | bytes 294920 | tf_op jit(solution)/shard_map/ppermute | solution.py:16
  414.8 11.8 %collective-permute-start.24 = (f32[3,34,1,256]{3,1,2,0:T(8,128)S(1)}, f32[3,34,1,256]{3,1,2,0:T(8,128)S(1)}, u32[]{:S(2)}, u32[]{:S(2)}) collective-permute-start(f32[3,34,1,256]{3,1,2,0:T(8,128)S(1)} %copy.84), channel_id=1, source_target_pairs={{8,0},{16,8},{24,16},{9,1},{17,9},{25,17},{10,2},{18,10},{26,18},{... | collective-permute-start | bytes 313352 | tf_op jit(solution)/shard_map/ppermute | solution.py:27
  416.1 10.7 %collective-permute-start.23 = (f32[3,34,1,256]{3,1,2,0:T(8,128)S(1)}, f32[3,34,1,256]{3,1,2,0:T(8,128)S(1)}, u32[]{:S(2)}, u32[]{:S(2)}) collective-permute-start(f32[3,34,1,256]{3,1,2,0:T(8,128)S(1)} %copy.82), channel_id=1, source_target_pairs={{0,8},{8,16},{16,24},{1,9},{9,17},{17,25},{2,10},{10,18},{18,26},{... | collective-permute-start | bytes 313352 | tf_op jit(solution)/shard_map/ppermute | solution.py:24
  420.9 5.6 collective-permute-start.34
  435.3 24.7 %collective-permute-start.26 = (f32[3,34,34,1]{2,1,3,0:T(8,128)S(1)}, f32[3,34,34,1]{2,1,3,0:T(8,128)S(1)}, u32[]{:S(2)}, u32[]{:S(2)}) collective-permute-start(f32[3,34,34,1]{2,1,3,0:T(8,128)S(1)} %copy.90), channel_id=1, source_target_pairs={{1,0},{2,1},{3,2},{4,3},{5,4},{6,5},{7,6},{9,8},{10,9},{11,10},{12... | collective-permute-start | bytes 41624 | tf_op jit(solution)/shard_map/ppermute | solution.py:27
  440.9 16.8 %collective-permute-start.25 = (f32[3,34,34,1]{2,1,3,0:T(8,128)S(1)}, f32[3,34,34,1]{2,1,3,0:T(8,128)S(1)}, u32[]{:S(2)}, u32[]{:S(2)}) collective-permute-start(f32[3,34,34,1]{2,1,3,0:T(8,128)S(1)} %copy.88), channel_id=1, source_target_pairs={{0,1},{1,2},{2,3},{3,4},{4,5},{5,6},{6,7},{8,9},{9,10},{10,11},{11... | collective-permute-start | bytes 41624 | tf_op jit(solution)/shard_map/ppermute | solution.py:24
  450.0 5.5 collective-permute-start.35
  462.1 19.1 %copy-start.9 = (f32[3,32,32,256]{3,2,1,0:T(8,128)S(1)}, f32[3,32,32,256]{3,2,1,0:T(8,128)}, u32[]{:S(2)}) copy-start(f32[3,32,32,256]{3,2,1,0:T(8,128)} %get-tuple-element.29) | copy-start | bytes 9437188
  462.1 19.1 %copy-start.16 = (f32[3,33,33,1]{3,2,1,0:T(8,128)S(1)}, f32[3,33,33,1]{3,2,1,0:T(8,128)}, u32[]{:S(2)}) copy-start(f32[3,33,33,1]{3,2,1,0:T(8,128)} %copy.105) | copy-start | bytes 39208
  476.6 18.2 %copy-start.7 = (f32[3,32,32,256]{3,2,1,0:T(8,128)}, f32[3,32,32,256]{3,2,1,0:T(8,128)S(1)}, u32[]{:S(2)}) copy-start(f32[3,32,32,256]{3,2,1,0:T(8,128)S(1)} %fusion.48) | copy-start | bytes 9437188
  476.6 9.3 %collective-permute-start.27 = (f32[3,1,32,256]{3,2,1,0:T(8,128)S(1)}, f32[3,1,32,256]{3,2,1,0:T(8,128)S(1)}, u32[]{:S(2)}, u32[]{:S(2)}) collective-permute-start(f32[3,1,32,256]{3,2,1,0:T(8,128)S(1)} %get-tuple-element.64), channel_id=1, source_target_pairs={{0,32},{32,64},{64,96},{1,33},{33,65},{65,97},{2,34},{34,66},{66,9... | collective-permute-start | bytes 294920 | tf_op jit(solution)/shard_map/ppermute | solution.py:24
  479.9 6.0 collective-permute-start.28
  486.1 8.4 %collective-permute-start.30 = (f32[3,34,1,256]{3,1,2,0:T(8,128)S(1)}, f32[3,34,1,256]{3,1,2,0:T(8,128)S(1)}, u32[]{:S(2)}, u32[]{:S(2)}) collective-permute-start(f32[3,34,1,256]{3,1,2,0:T(8,128)S(1)} %copy.94), channel_id=1, source_target_pairs={{8,0},{16,8},{24,16},{9,1},{17,9},{25,17},{10,2},{18,10},{26,18},{... | collective-permute-start | bytes 313352 | tf_op jit(solution)/shard_map/ppermute | solution.py:27
  487.4 7.2 %collective-permute-start.29 = (f32[3,34,1,256]{3,1,2,0:T(8,128)S(1)}, f32[3,34,1,256]{3,1,2,0:T(8,128)S(1)}, u32[]{:S(2)}, u32[]{:S(2)}) collective-permute-start(f32[3,34,1,256]{3,1,2,0:T(8,128)S(1)} %copy.92), channel_id=1, source_target_pairs={{0,8},{8,16},{16,24},{1,9},{9,17},{17,25},{2,10},{10,18},{18,26},{... | collective-permute-start | bytes 313352 | tf_op jit(solution)/shard_map/ppermute | solution.py:24
  504.5 29.0 %collective-permute-start.32 = (f32[3,34,34,1]{2,1,3,0:T(8,128)}, f32[3,34,34,1]{2,1,3,0:T(8,128)}, u32[]{:S(2)}, u32[]{:S(2)}) collective-permute-start(f32[3,34,34,1]{2,1,3,0:T(8,128)} %copy.100), channel_id=1, source_target_pairs={{1,0},{2,1},{3,2},{4,3},{5,4},{6,5},{7,6},{9,8},{10,9},{11,10},{12... | collective-permute-start | bytes 41624 | tf_op jit(solution)/shard_map/ppermute | solution.py:27
  506.4 24.0 %collective-permute-start.31 = (f32[3,34,34,1]{2,1,3,0:T(8,128)}, f32[3,34,34,1]{2,1,3,0:T(8,128)}, u32[]{:S(2)}, u32[]{:S(2)}) collective-permute-start(f32[3,34,34,1]{2,1,3,0:T(8,128)} %copy.98), channel_id=1, source_target_pairs={{0,1},{1,2},{2,3},{3,4},{4,5},{5,6},{6,7},{8,9},{9,10},{10,11},{11... | collective-permute-start | bytes 41624 | tf_op jit(solution)/shard_map/ppermute | solution.py:24
  536.4 16.5 %copy-start.1 = (f32[32,32,256]{2,1,0:T(8,128)S(1)}, f32[32,32,256]{2,1,0:T(8,128)}, u32[]{:S(2)}) copy-start(f32[32,32,256]{2,1,0:T(8,128)} %param.7) | copy-start | bytes 3145732
  536.4 16.5 %copy-start.10 = (f32[1,32,32,256]{3,2,1,0:T(8,128)S(1)}, f32[1,32,32,256]{3,2,1,0:T(8,128)}, u32[]{:S(2)}) copy-start(f32[1,32,32,256]{3,2,1,0:T(8,128)} %fusion.119) | copy-start | bytes 3145732
  552.9 7.9 %collective-permute-start.36 = (f32[5,1,32,256]{3,2,1,0:T(8,128)S(1)}, f32[5,1,32,256]{3,2,1,0:T(8,128)S(1)}, u32[]{:S(2)}, u32[]{:S(2)}) collective-permute-start(f32[5,1,32,256]{3,2,1,0:T(8,128)S(1)} %get-tuple-element.42), channel_id=1, source_target_pairs={{0,32},{32,64},{64,96},{1,33},{33,65},{65,97},{2,34},{34,66},{66,9... | collective-permute-start | bytes 491528 | tf_op jit(solution)/shard_map/ppermute | solution.py:24
  556.9 8.0 %collective-permute-start.37 = (f32[5,1,32,256]{3,2,1,0:T(8,128)S(1)}, f32[5,1,32,256]{3,2,1,0:T(8,128)S(1)}, u32[]{:S(2)}, u32[]{:S(2)}) collective-permute-start(f32[5,1,32,256]{3,2,1,0:T(8,128)S(1)} %get-tuple-element.43), channel_id=1, source_target_pairs={{32,0},{64,32},{96,64},{33,1},{65,33},{97,65},{34,2},{66,34},{98,6... | collective-permute-start | bytes 491528 | tf_op jit(solution)/shard_map/ppermute | solution.py:27
  565.2 6.6 %collective-permute-start.38 = (f32[5,34,1,256]{3,2,1,0:T(1,128)S(1)}, f32[5,34,1,256]{3,2,1,0:T(1,128)S(1)}, u32[]{:S(2)}, u32[]{:S(2)}) collective-permute-start(f32[5,34,1,256]{3,2,1,0:T(1,128)S(1)} %get-tuple-element.40), channel_id=1, source_target_pairs={{0,8},{8,16},{16,24},{1,9},{9,17},{17,25},{2,10},{10,18},{18,26},{... | collective-permute-start | bytes 522248 | tf_op jit(solution)/shard_map/ppermute | solution.py:24
  568.5 7.1 %collective-permute-start.39 = (f32[5,34,1,256]{3,2,1,0:T(1,128)S(1)}, f32[5,34,1,256]{3,2,1,0:T(1,128)S(1)}, u32[]{:S(2)}, u32[]{:S(2)}) collective-permute-start(f32[5,34,1,256]{3,2,1,0:T(1,128)S(1)} %get-tuple-element.41), channel_id=1, source_target_pairs={{8,0},{16,8},{24,16},{9,1},{17,9},{25,17},{10,2},{18,10},{26,18},{... | collective-permute-start | bytes 522248 | tf_op jit(solution)/shard_map/ppermute | solution.py:27
  571.8 5.4 copy-start.17
  584.5 9.2 %collective-permute-start.41 = (f32[5,34,34,1]{2,3,1,0:T(1,128)}, f32[5,34,34,1]{2,3,1,0:T(1,128)}, u32[]{:S(2)}, u32[]{:S(2)}) collective-permute-start(f32[5,34,34,1]{2,3,1,0:T(1,128)} %copy.107), channel_id=1, source_target_pairs={{1,0},{2,1},{3,2},{4,3},{5,4},{6,5},{7,6},{9,8},{10,9},{11,10},{12... | collective-permute-start | bytes 69368 | tf_op jit(solution)/shard_map/ppermute | solution.py:27
  591.6 5.6 collective-permute-start.40
  621.0 6.0 copy-start.2
  621.0 6.0 copy-start.11
  621.0 6.0 copy-start.12
  621.0 6.1 copy-start.13
  621.0 6.1 copy-start.18
  621.0 6.1 copy-start.20
  (3 other events, 5.3 us)
where the time goes:
time: 647 us; the launch traced here: 638 us
  blocking collectives  192 us (30%)
  other arithmetic  178 us (28%)
  starting transfers between devices  118 us (18%)
  local copies, waits for them, and re-layouts  98.8 us (15%)
  waiting for transfers between devices  49.5 us (8%)
    psum x2, blocking collectives, squares(): return lax.psum(inner(residual, residual), ('bx', 'by', 'bz'))  128 us
    ppermute x18, starting transfers between devices, padded(): lax.ppermute(lax.slice_in_dim(block, block.shape[dim] - width, None, axis...  64.5 us
    psum x1, blocking collectives, on_device(): alpha = norm_now / lax.psum(inner(direction, image), ('bx', 'by', 'bz'))  63.9 us
    ppermute x18, starting transfers between devices, padded(): lax.ppermute(lax.slice_in_dim(block, 0, width, axis=dim), axis, backward)  36.5 us
    reduce_sum x3, other arithmetic, inner(): return jnp.sum(first * second, axis=(1, 2, 3), keepdims=True)  34.7 us
    slice x19, local copies, waits for them, and re-layouts, padded(): lax.slice_in_dim(block, block.shape[dim] - width, None, axis=dim)  30.9 us
    ppermute x18, waiting for transfers between devices, padded(): lax.ppermute(lax.slice_in_dim(block, 0, width, axis=dim), axis, backward)  30.7 us
    add x2, other arithmetic, one_sweep(): return relaxed + RELAX_RATE * free * (neighbours(extended) / 6.0 - relaxed)  28.6 us
  transfers between devices with their start and end apart: 42, of which 22 were waited for; matrix products, arithmetic and copies ran while one was open for 11% of the time, Pallas kernels for 0%

commit v1 on v0

--- a/solution.py
+++ b/solution.py
@@ -143,7 +143,7 @@
 
 
 def squares(residual):
-    return lax.psum(inner(residual, residual), ("bx", "by", "bz"))
+    return lax.psum(lax.psum(inner(residual, residual), ("by", "bz")), "bx")
 
 
 def one_sweep(relaxed, free):

time: 647 us -> 726 us (1.12)
  blocking collectives: 192 us -> 268 us
    psum x1 -> x2, blocking collectives: 63.9 us -> 128 us  [on_device(): alpha = norm_now / lax.psum(inner(direction, image), ('bx', 'by', 'bz'))]
    psum x2 -> x4, blocking collectives: 128 us -> 139 us  [squares(): return lax.psum(lax.psum(inner(residual, residual), ('by', 'bz')), 'bx')]
  transfers between devices with their start and end apart: 42 -> 42, of which waited for: 22 -> 21; matrix products, arithmetic and copies ran while one was open for 11% -> 10% of each run, Pallas kernels for 0% -> 0%
where the time goes in v1:
time: 726 us; the launch traced here: 717 us
  blocking collectives  268 us (37%)
  other arithmetic  178 us (25%)
  starting transfers between devices  120 us (17%)
  local copies, waits for them, and re-layouts  98.9 us (14%)
  waiting for transfers between devices  49.6 us (7%)
    psum x4, blocking collectives, squares(): return lax.psum(lax.psum(inner(residual, residual), ('by', 'bz')), 'bx')  139 us
    psum x2, blocking collectives, on_device(): alpha = norm_now / lax.psum(inner(direction, image), ('bx', 'by', 'bz'))  128 us
    ppermute x18, starting transfers between devices, padded(): lax.ppermute(lax.slice_in_dim(block, block.shape[dim] - width, None, axis...  63.7 us
    ppermute x18, starting transfers between devices, padded(): lax.ppermute(lax.slice_in_dim(block, 0, width, axis=dim), axis, backward)  39.3 us
    reduce_sum x3, other arithmetic, inner(): return jnp.sum(first * second, axis=(1, 2, 3), keepdims=True)  34.8 us
    slice x19, local copies, waits for them, and re-layouts, padded(): lax.slice_in_dim(block, block.shape[dim] - width, None, axis=dim)  30.9 us
    ppermute x18, waiting for transfers between devices, padded(): lax.ppermute(lax.slice_in_dim(block, 0, width, axis=dim), axis, backward)  30.7 us
    add x2, other arithmetic, one_sweep(): return relaxed + RELAX_RATE * free * (neighbours(extended) / 6.0 - relaxed)  29 us
  transfers between devices with their start and end apart: 42, of which 21 were waited for; matrix products, arithmetic and copies ran while one was open for 10% of the time, Pallas kernels for 0%

profile of v1, /device:TPU:1, one launch (start us, length us, event | category | flops | bytes accessed | tf_op | source)
XLA Modules:
  0.0 716.7 jit_solution(15859905743366558238)
XLA Ops:
  1.6 4.0 collective-permute-start
  8.0 3.1 collective-permute-start.1
  14.1 5.8 collective-permute-start.2
  22.3 3.6 select_maximum_fusion.3
  29.0 4.0 collective-permute-start.3
  34.6 3.7 collective-permute-done.4
  38.5 4.0 collective-permute-start.5
  45.3 4.1 collective-permute-done.6
  52.9 3.0 copy.64
  55.9 3.0 copy.66
  61.2 5.9 collective-permute-start.7
  67.1 7.7 %fusion.120 = f32[32,32,256]{2,1,0:T(8,128)} fusion(f32[34,34,258]{2,1,0:T(8,128)} %slice_bitcast_fusion.7), kind=kLoop, calls=%fused_computation.316 | loop fusion | flops 2097152 | bytes 9437184 | tf_op jit(solution)/shard_map/mul | solution.py:72
  80.7 16.0 %multiply_reduce_fusion.1 = (f32[3]{0:T(128)}, f32[3]{0:T(128)}, f32[3,32,32,256]{3,2,1,0:T(8,128)}) fusion(f32[1,32,32,256]{3,2,1,0:T(8,128)} %copy-done.4, f32[1,32,32,256]{3,2,1,0:T(8,128)S(1)} %multiply_bitcast_fusion.1, f32[1,32,32,256]{3,2,1,0:T(8,128)S(1)} %get-tuple-element.80, f32[3,34,34,1]{3,2,1,0:T(8,128)} %copy.67, ...), kind=kLoop, calls=%fused_computation.195 | loop fusion | flops 36175864 | bytes 7773304 | tf_op jit(solution)/shard_map/reduce_sum | solution.py:117
  96.7 61.0 %psum.42 = f32[3,1,1,1]{0,3,2,1:T(1,128)S(1)} all-reduce(f32[3,1,1,1]{0,3,2,1:T(1,128)} %bitcast.58), channel_id=1, replica_groups=mesh['bx'=4,'by'=4,'bz'=8] {'by','bz'}, use_global_device_ids=true, to_apply=%region_1.2 | all-reduce | flops 3 | bytes 24 | tf_op jit(solution)/shard_map/psum | solution.py:146
  157.7 66.5 %psum.44 = f32[3,1,1,1]{0,3,2,1:T(1,128)S(1)} all-reduce(f32[3,1,1,1]{0,3,2,1:T(1,128)} %bitcast.57), channel_id=1, replica_groups=mesh['bx'=4,'by'=4,'bz'=8] {'bx','by','bz'}, use_global_device_ids=true, to_apply=%region_4.5 | all-reduce | flops 3 | bytes 24 | tf_op jit(solution)/shard_map/psum | solution.py:164
  224.2 6.7 psum.43
  233.8 64.9 %psum.45 = f32[3,1,1,1]{0,3,2,1:T(1,128)S(1)} all-reduce(f32[3,1,1,1]{0,3,2,1:T(1,128)S(1)} %bitcast.60), channel_id=1, replica_groups=mesh['bx'=4,'by'=4,'bz'=8] {'by','bz'}, use_global_device_ids=true, to_apply=%region_6.7 | all-reduce | flops 3 | bytes 24 | tf_op jit(solution)/shard_map/psum | solution.py:146
  298.7 6.6 psum.46
  305.4 3.1 multiply_add_fusion.3
  312.9 3.7 collective-permute-done.10
  319.7 3.8 collective-permute-done.12
  326.9 3.0 copy.68
  329.9 3.2 collective-permute-start.13
  333.1 3.0 copy.70
  336.1 6.0 collective-permute-start.14
  348.0 15.8 %fusion.67 = f32[3]{0:T(128)} fusion(f32[3,32,32,256]{3,2,1,0:T(8,128)} %copy-done.5, f32[3,34,34,1]{3,2,1,0:T(8,128)} %copy.71, f32[3,34,1,256]{3,2,1,0:T(1,128)S(1)} %collective-permute-done.12, f32[3,34,1,256]{3,2,1,0:T(1,128)S(1)} %collective-permute-done.11, f32[3,1,32,256]{3,2,1,0:T(8,128)S(1)} %collective-permute-done.10, ...), kind=kLoop, calls=%fused_computation.147 | loop fusion | flops 23592956 | bytes 4627564 | tf_op jit(solution)/shard_map/reduce_sum | solution.py:117
  363.9 61.9 %psum.47 = f32[3,1,1,1]{0,3,2,1:T(1,128)S(1)} all-reduce(f32[3,1,1,1]{0,3,2,1:T(1,128)} %bitcast.59), channel_id=1, replica_groups=mesh['bx'=4,'by'=4,'bz'=8] {'bx','by','bz'}, use_global_device_ids=true, to_apply=%region_9.10 | all-reduce | flops 3 | bytes 24 | tf_op jit(solution)/shard_map/psum | solution.py:164
  426.4 6.8 multiply_add_fusion
  437.8 3.7 collective-permute-done.16
  443.0 4.0 collective-permute-start.17
  451.7 3.1 copy.78
  456.4 5.5 collective-permute-start.20
  469.8 14.2 %fusion.57 = f32[3,32,32,256]{3,2,1,0:T(8,128)S(1)} fusion(f32[3,32,32,256]{3,2,1,0:T(8,128)} %copy-done.3, f32[3,34,34,1]{3,2,1,0:T(8,128)} %copy.81, f32[3,34,1,256]{3,2,1,0:T(1,128)S(1)} %copy.75, f32[3,34,1,256]{3,2,1,0:T(1,128)S(1)} %copy.73, f32[3,1,32,256]{3,2,1,0:T(8,128)S(1)} %collective-permute-done.16, ...), kind=kLoop, calls=%fused_computation.119 | loop fusion | flops 21233664 | bytes 7773280 | tf_op jit(solution)/shard_map/add | solution.py:151
  489.0 3.5 collective-permute-done.22
  493.9 4.7 collective-permute-start.23
  500.0 4.3 collective-permute-done.34
  513.1 4.5 collective-permute-start.26
  517.6 4.0 collective-permute-start.25
  529.0 3.6 collective-permute-done.35
  539.1 14.9 %fusion.48 = f32[3,32,32,256]{3,2,1,0:T(8,128)S(1)} fusion(f32[3,32,32,256]{3,2,1,0:T(8,128)} %copy-done.6, f32[3,34,34,1]{3,2,1,0:T(8,128)} %copy.91, f32[3,34,1,256]{3,2,1,0:T(1,128)S(1)} %copy.85, f32[3,34,1,256]{3,2,1,0:T(1,128)S(1)} %copy.83, f32[3,1,32,256]{3,2,1,0:T(8,128)S(1)} %collective-permute-done.22, ...), kind=kLoop, calls=%fused_computation.92 | loop fusion | flops 21233664 | bytes 7773280 | tf_op jit(solution)/shard_map/add | solution.py:151
  558.2 4.7 select_maximum_fusion
  564.5 4.7 collective-permute-start.29
  575.2 3.1 copy.98
  578.3 3.1 copy.100
  583.4 3.6 collective-permute-start.31
  587.0 20.1 %fusion.119 = f32[1,32,32,256]{3,2,1,0:T(8,128)} fusion(f32[32,32,256]{2,1,0:T(8,128)S(1)} %copy-done, f32[32,32,256]{2,1,0:T(8,128)} %param.8, f32[34,34,258]{2,1,0:T(8,128)} %get-tuple-element.37, f32[34,34,258]{2,1,0:T(8,128)} %get-tuple-element.36, f32[34,34,258]{2,1,0:T(8,128)S(1)} %get-tuple-element.35), kind=kLoop, calls=%fused_computation.292 | loop fusion | flops 8126464 | bytes 28311552 | tf_op jit(solution)/shard_map/broadcast_in_dim | solution.py:181
  607.2 3.0 copy.99
  610.2 3.0 copy.101
  613.2 16.4 %fusion.127 = (f32[3,32,32,256]{3,2,1,0:T(8,128)S(1)}, f32[3,32,32,256]{3,2,1,0:T(8,128)}) fusion(f32[3,32,32,256]{3,2,1,0:T(8,128)} %copy-done.3, f32[3,32,32,256]{3,2,1,0:T(8,128)} %copy-done.7, f32[3,34,34,1]{3,2,1,0:T(8,128)} %copy.101, f32[3,34,1,256]{3,2,1,0:T(1,128)S(1)} %copy.95, f32[3,1,32,256]{3,2,1,0:T(8,128)S(1)} %collective-permute-done.28, ...), kind=kLoop, calls=%fused_computation.365 | loop fusion | flops 22020096 | bytes 14064736 | tf_op jit(solution)/shard_map/sub | solution.py:181
  629.6 4.0 collective-permute-start.36
  637.5 4.1 collective-permute-done.37
  641.9 3.4 collective-permute-start.38
  648.6 3.8 collective-permute-done.39
  654.0 3.9 fusion.130
  657.9 3.5 copy.107
  661.4 3.4 collective-permute-start.41
  664.8 3.5 copy.106
  668.3 4.0 collective-permute-start.40
  672.3 3.5 copy.109
  675.8 3.5 copy.108
  679.3 16.1 %pad_maximum_fusion = f32[5,34,34,258]{3,2,1,0:T(8,128)S(1)} fusion(f32[5,34,34,1]{3,2,1,0:T(8,128)} %copy.109, f32[5,34,1,256]{3,2,1,0:T(1,128)} %copy-done.19, f32[5,1,32,256]{3,2,1,0:T(8,128)S(1)} %collective-permute-done.37, f32[1,32,32,256]{3,2,1,0:T(8,128)} %fusion.119, f32[1,32,32,256]{3,2,1,0:T(8,128)} %bitcast.46, ...), kind=kLoop, calls=%fused_computation | loop fusion | flops 11929920 | bytes 11929920 | tf_op jit(solution)/shard_map/concatenate | solution.py:28
  695.8 3.7 broadcast_compare_fusion.5
  699.6 6.0 broadcast_compare_fusion.1
  705.7 9.3 %fusion.84 = f32[2,32,32,256]{3,2,1,0:T(8,128)S(1)} fusion(f32[3,32,32,256]{3,2,1,0:T(8,128)S(1)} %get-tuple-element.24, f32[1,32,32,256]{3,2,1,0:T(8,128)S(1)} %bitcast.52, f32[5,34,34,1]{3,2,1,0:T(8,128)S(1)} %copy-done.13, f32[5,34,1,256]{3,2,1,0:T(1,128)S(1)} %copy-done.20, f32[5,34,1,256]{3,2,1,0:T(1,128)S(1)} %copy-done.18, ...), kind=kLoop, calls=%fused_computation.206 | loop fusion | flops 25690112 | bytes 15926432 | tf_op jit(solution)/shard_map/sub | solution.py:112
  (176 shorter events, 123.2 us)
Async XLA Ops:
  0.6 12.5 %copy-start.14 = (f32[32,32,256]{2,1,0:T(8,128)S(1)}, f32[32,32,256]{2,1,0:T(8,128)}, u32[]{:S(2)}) copy-start(f32[32,32,256]{2,1,0:T(8,128)} %param.8) | copy-start | bytes 3145732
  0.6 12.5 %copy-start = (f32[32,32,256]{2,1,0:T(8,128)S(1)}, f32[32,32,256]{2,1,0:T(8,128)}, u32[]{:S(2)}) copy-start(f32[32,32,256]{2,1,0:T(8,128)} %param.7) | copy-start | bytes 3145732
  1.6 5.3 collective-permute-start
  8.0 4.5 collective-permute-start.1
  14.1 6.8 collective-permute-start.2
  28.7 21.6 %copy-start.4 = (f32[1,32,32,256]{3,2,1,0:T(8,128)}, f32[1,32,32,256]{3,2,1,0:T(8,128)S(1)}, u32[]{:S(2)}) copy-start(f32[1,32,32,256]{3,2,1,0:T(8,128)S(1)} %get-tuple-element.81) | copy-start | bytes 3145732
  29.0 5.6 collective-permute-start.3
  33.0 5.4 collective-permute-start.4
  38.5 6.8 collective-permute-start.5
  42.5 6.8 collective-permute-start.6
  58.9 18.8 %collective-permute-start.8 = (f32[3,34,34,1]{2,3,1,0:T(1,128)}, f32[3,34,34,1]{2,3,1,0:T(1,128)}, u32[]{:S(2)}, u32[]{:S(2)}) collective-permute-start(f32[3,34,34,1]{2,3,1,0:T(1,128)} %copy.66), channel_id=1, source_target_pairs={{1,0},{2,1},{3,2},{4,3},{5,4},{6,5},{7,6},{9,8},{10,9},{11,10},{12... | collective-permute-start | bytes 41624 | tf_op jit(solution)/shard_map/ppermute | solution.py:27
  61.2 13.6 %collective-permute-start.7 = (f32[3,34,34,1]{2,3,1,0:T(1,128)}, f32[3,34,34,1]{2,3,1,0:T(1,128)}, u32[]{:S(2)}, u32[]{:S(2)}) collective-permute-start(f32[3,34,34,1]{2,3,1,0:T(1,128)} %copy.64), channel_id=1, source_target_pairs={{0,1},{1,2},{2,3},{3,4},{4,5},{5,6},{6,7},{8,9},{9,10},{10,11},{11... | collective-permute-start | bytes 41624 | tf_op jit(solution)/shard_map/ppermute | solution.py:24
  230.9 74.5 %copy-start.22 = (f32[3]{0:T(128)}, f32[3]{0:T(128)S(1)}, u32[]{:S(2)}) copy-start(f32[3]{0:T(128)S(1)} %divide_bitcast_fusion.2) | copy-start | bytes 40
  305.4 3.1 copy-start.24
  308.5 15.7 %copy-start.5 = (f32[3,32,32,256]{3,2,1,0:T(8,128)}, f32[3,32,32,256]{3,2,1,0:T(8,128)S(1)}, u32[]{:S(2)}) copy-start(f32[3,32,32,256]{3,2,1,0:T(8,128)S(1)} %multiply_add_fusion.3) | copy-start | bytes 9437188
  308.5 4.3 collective-permute-start.9
  311.2 5.4 collective-permute-start.10
  316.8 3.0 collective-permute-start.11
  318.1 5.4 collective-permute-start.12
  329.9 12.2 %collective-permute-start.13 = (f32[3,34,34,1]{2,3,1,0:T(1,128)}, f32[3,34,34,1]{2,3,1,0:T(1,128)}, u32[]{:S(2)}, u32[]{:S(2)}) collective-permute-start(f32[3,34,34,1]{2,3,1,0:T(1,128)} %copy.68), channel_id=1, source_target_pairs={{0,1},{1,2},{2,3},{3,4},{4,5},{5,6},{6,7},{8,9},{9,10},{10,11},{11... | collective-permute-start | bytes 41624 | tf_op jit(solution)/shard_map/ppermute | solution.py:24
  336.1 9.0 %collective-permute-start.14 = (f32[3,34,34,1]{2,3,1,0:T(1,128)}, f32[3,34,34,1]{2,3,1,0:T(1,128)}, u32[]{:S(2)}, u32[]{:S(2)}) collective-permute-start(f32[3,34,34,1]{2,3,1,0:T(1,128)} %copy.70), channel_id=1, source_target_pairs={{1,0},{2,1},{3,2},{4,3},{5,4},{6,5},{7,6},{9,8},{10,9},{11,10},{12... | collective-permute-start | bytes 41624 | tf_op jit(solution)/shard_map/ppermute | solution.py:27
  433.2 18.4 %copy-start.3 = (f32[3,32,32,256]{3,2,1,0:T(8,128)}, f32[3,32,32,256]{3,2,1,0:T(8,128)S(1)}, u32[]{:S(2)}) copy-start(f32[3,32,32,256]{3,2,1,0:T(8,128)S(1)} %get-tuple-element.26) | copy-start | bytes 9437188
  433.3 4.5 collective-permute-start.15
  436.1 5.4 collective-permute-start.16
  441.7 5.6 collective-permute-start.18
  443.0 5.8 collective-permute-start.17
  456.4 11.3 %collective-permute-start.20 = (f32[3,34,34,1]{2,1,3,0:T(8,128)}, f32[3,34,34,1]{2,1,3,0:T(8,128)S(1)}, u32[]{:S(2)}, u32[]{:S(2)}) collective-permute-start(f32[3,34,34,1]{2,1,3,0:T(8,128)} %copy.80), channel_id=1, source_target_pairs={{1,0},{2,1},{3,2},{4,3},{5,4},{6,5},{7,6},{9,8},{10,9},{11,10},{12... | collective-permute-start | bytes 41624 | tf_op jit(solution)/shard_map/ppermute | solution.py:27
  461.9 3.5 collective-permute-start.19
  465.4 73.7 %copy-start.15 = (f32[32,32,256]{2,1,0:T(8,128)}, f32[32,32,256]{2,1,0:T(8,128)S(1)}, u32[]{:S(2)}) copy-start(f32[32,32,256]{2,1,0:T(8,128)S(1)} %subtract_multiply_fusion) | copy-start | bytes 3145732
  469.8 17.8 %copy-start.8 = (f32[3,32,32,256]{3,2,1,0:T(8,128)S(1)}, f32[3,32,32,256]{3,2,1,0:T(8,128)}, u32[]{:S(2)}) copy-start(f32[3,32,32,256]{3,2,1,0:T(8,128)} %get-tuple-element.27) | copy-start | bytes 9437188
  484.0 20.7 %copy-start.6 = (f32[3,32,32,256]{3,2,1,0:T(8,128)}, f32[3,32,32,256]{3,2,1,0:T(8,128)S(1)}, u32[]{:S(2)}) copy-start(f32[3,32,32,256]{3,2,1,0:T(8,128)S(1)} %fusion.57) | copy-start | bytes 9437188
  484.1 4.9 collective-permute-start.21
  486.3 6.1 collective-permute-start.22
  487.7 11.0 %collective-permute-start.33 = (f32[3,1,32,256]{3,2,1,0:T(8,128)S(1)}, f32[3,1,32,256]{3,2,1,0:T(8,128)S(1)}, u32[]{:S(2)}, u32[]{:S(2)}) collective-permute-start(f32[3,1,32,256]{3,2,1,0:T(8,128)S(1)} %slice.782), channel_id=1, source_target_pairs={{32,0},{64,32},{96,64},{33,1},{65,33},{97,65},{34,2},{66,34},{98,6... | collective-permute-start | bytes 294920 | tf_op jit(solution)/shard_map/ppermute | solution.py:16
  492.6 11.8 %collective-permute-start.24 = (f32[3,34,1,256]{3,1,2,0:T(8,128)S(1)}, f32[3,34,1,256]{3,1,2,0:T(8,128)S(1)}, u32[]{:S(2)}, u32[]{:S(2)}) collective-permute-start(f32[3,34,1,256]{3,1,2,0:T(8,128)S(1)} %copy.84), channel_id=1, source_target_pairs={{8,0},{16,8},{24,16},{9,1},{17,9},{25,17},{10,2},{18,10},{26,18},{... | collective-permute-start | bytes 313352 | tf_op jit(solution)/shard_map/ppermute | solution.py:27
  493.9 10.7 %collective-permute-start.23 = (f32[3,34,1,256]{3,1,2,0:T(8,128)S(1)}, f32[3,34,1,256]{3,1,2,0:T(8,128)S(1)}, u32[]{:S(2)}, u32[]{:S(2)}) collective-permute-start(f32[3,34,1,256]{3,1,2,0:T(8,128)S(1)} %copy.82), channel_id=1, source_target_pairs={{0,8},{8,16},{16,24},{1,9},{9,17},{17,25},{2,10},{10,18},{18,26},{... | collective-permute-start | bytes 313352 | tf_op jit(solution)/shard_map/ppermute | solution.py:24
  498.7 5.6 collective-permute-start.34
  513.1 23.8 %collective-permute-start.26 = (f32[3,34,34,1]{2,1,3,0:T(8,128)S(1)}, f32[3,34,34,1]{2,1,3,0:T(8,128)S(1)}, u32[]{:S(2)}, u32[]{:S(2)}) collective-permute-start(f32[3,34,34,1]{2,1,3,0:T(8,128)S(1)} %copy.90), channel_id=1, source_target_pairs={{1,0},{2,1},{3,2},{4,3},{5,4},{6,5},{7,6},{9,8},{10,9},{11,10},{12... | collective-permute-start | bytes 41624 | tf_op jit(solution)/shard_map/ppermute | solution.py:27
  517.6 17.1 %collective-permute-start.25 = (f32[3,34,34,1]{2,1,3,0:T(8,128)S(1)}, f32[3,34,34,1]{2,1,3,0:T(8,128)S(1)}, u32[]{:S(2)}, u32[]{:S(2)}) collective-permute-start(f32[3,34,34,1]{2,1,3,0:T(8,128)S(1)} %copy.88), channel_id=1, source_target_pairs={{0,1},{1,2},{2,3},{3,4},{4,5},{5,6},{6,7},{8,9},{9,10},{10,11},{11... | collective-permute-start | bytes 41624 | tf_op jit(solution)/shard_map/ppermute | solution.py:24
  527.0 5.5 collective-permute-start.35
  539.1 19.1 %copy-start.9 = (f32[3,32,32,256]{3,2,1,0:T(8,128)S(1)}, f32[3,32,32,256]{3,2,1,0:T(8,128)}, u32[]{:S(2)}) copy-start(f32[3,32,32,256]{3,2,1,0:T(8,128)} %get-tuple-element.27) | copy-start | bytes 9437188
  539.1 19.1 %copy-start.16 = (f32[3,33,33,1]{3,2,1,0:T(8,128)S(1)}, f32[3,33,33,1]{3,2,1,0:T(8,128)}, u32[]{:S(2)}) copy-start(f32[3,33,33,1]{3,2,1,0:T(8,128)} %copy.105) | copy-start | bytes 39208
  554.0 17.8 %copy-start.7 = (f32[3,32,32,256]{3,2,1,0:T(8,128)}, f32[3,32,32,256]{3,2,1,0:T(8,128)S(1)}, u32[]{:S(2)}) copy-start(f32[3,32,32,256]{3,2,1,0:T(8,128)S(1)} %fusion.48) | copy-start | bytes 9437188
  554.0 8.9 %collective-permute-start.27 = (f32[3,1,32,256]{3,2,1,0:T(8,128)S(1)}, f32[3,1,32,256]{3,2,1,0:T(8,128)S(1)}, u32[]{:S(2)}, u32[]{:S(2)}) collective-permute-start(f32[3,1,32,256]{3,2,1,0:T(8,128)S(1)} %get-tuple-element.62), channel_id=1, source_target_pairs={{0,32},{32,64},{64,96},{1,33},{33,65},{65,97},{2,34},{34,66},{66,9... | collective-permute-start | bytes 294920 | tf_op jit(solution)/shard_map/ppermute | solution.py:24
  556.9 6.0 collective-permute-start.28
  563.2 8.4 %collective-permute-start.30 = (f32[3,34,1,256]{3,1,2,0:T(8,128)S(1)}, f32[3,34,1,256]{3,1,2,0:T(8,128)S(1)}, u32[]{:S(2)}, u32[]{:S(2)}) collective-permute-start(f32[3,34,1,256]{3,1,2,0:T(8,128)S(1)} %copy.94), channel_id=1, source_target_pairs={{8,0},{16,8},{24,16},{9,1},{17,9},{25,17},{10,2},{18,10},{26,18},{... | collective-permute-start | bytes 313352 | tf_op jit(solution)/shard_map/ppermute | solution.py:27
  564.5 7.2 %collective-permute-start.29 = (f32[3,34,1,256]{3,1,2,0:T(8,128)S(1)}, f32[3,34,1,256]{3,1,2,0:T(8,128)S(1)}, u32[]{:S(2)}, u32[]{:S(2)}) collective-permute-start(f32[3,34,1,256]{3,1,2,0:T(8,128)S(1)} %copy.92), channel_id=1, source_target_pairs={{0,8},{8,16},{16,24},{1,9},{9,17},{17,25},{2,10},{10,18},{18,26},{... | collective-permute-start | bytes 313352 | tf_op jit(solution)/shard_map/ppermute | solution.py:24
  581.5 28.7 %collective-permute-start.32 = (f32[3,34,34,1]{2,1,3,0:T(8,128)}, f32[3,34,34,1]{2,1,3,0:T(8,128)}, u32[]{:S(2)}, u32[]{:S(2)}) collective-permute-start(f32[3,34,34,1]{2,1,3,0:T(8,128)} %copy.100), channel_id=1, source_target_pairs={{1,0},{2,1},{3,2},{4,3},{5,4},{6,5},{7,6},{9,8},{10,9},{11,10},{12... | collective-permute-start | bytes 41624 | tf_op jit(solution)/shard_map/ppermute | solution.py:27
  583.4 23.8 %collective-permute-start.31 = (f32[3,34,34,1]{2,1,3,0:T(8,128)}, f32[3,34,34,1]{2,1,3,0:T(8,128)}, u32[]{:S(2)}, u32[]{:S(2)}) collective-permute-start(f32[3,34,34,1]{2,1,3,0:T(8,128)} %copy.98), channel_id=1, source_target_pairs={{0,1},{1,2},{2,3},{3,4},{4,5},{5,6},{6,7},{8,9},{9,10},{10,11},{11... | collective-permute-start | bytes 41624 | tf_op jit(solution)/shard_map/ppermute | solution.py:24
  613.2 16.4 %copy-start.1 = (f32[32,32,256]{2,1,0:T(8,128)S(1)}, f32[32,32,256]{2,1,0:T(8,128)}, u32[]{:S(2)}) copy-start(f32[32,32,256]{2,1,0:T(8,128)} %param.7) | copy-start | bytes 3145732
  613.2 16.4 %copy-start.10 = (f32[1,32,32,256]{3,2,1,0:T(8,128)S(1)}, f32[1,32,32,256]{3,2,1,0:T(8,128)}, u32[]{:S(2)}) copy-start(f32[1,32,32,256]{3,2,1,0:T(8,128)} %fusion.119) | copy-start | bytes 3145732
  629.6 7.9 %collective-permute-start.36 = (f32[5,1,32,256]{3,2,1,0:T(8,128)S(1)}, f32[5,1,32,256]{3,2,1,0:T(8,128)S(1)}, u32[]{:S(2)}, u32[]{:S(2)}) collective-permute-start(f32[5,1,32,256]{3,2,1,0:T(8,128)S(1)} %get-tuple-element.40), channel_id=1, source_target_pairs={{0,32},{32,64},{64,96},{1,33},{33,65},{65,97},{2,34},{34,66},{66,9... | collective-permute-start | bytes 491528 | tf_op jit(solution)/shard_map/ppermute | solution.py:24
  633.6 8.0 %collective-permute-start.37 = (f32[5,1,32,256]{3,2,1,0:T(8,128)S(1)}, f32[5,1,32,256]{3,2,1,0:T(8,128)S(1)}, u32[]{:S(2)}, u32[]{:S(2)}) collective-permute-start(f32[5,1,32,256]{3,2,1,0:T(8,128)S(1)} %get-tuple-element.41), channel_id=1, source_target_pairs={{32,0},{64,32},{96,64},{33,1},{65,33},{97,65},{34,2},{66,34},{98,6... | collective-permute-start | bytes 491528 | tf_op jit(solution)/shard_map/ppermute | solution.py:27
  641.9 6.8 collective-permute-start.38
  645.3 7.2 %collective-permute-start.39 = (f32[5,34,1,256]{3,2,1,0:T(1,128)S(1)}, f32[5,34,1,256]{3,2,1,0:T(1,128)S(1)}, u32[]{:S(2)}, u32[]{:S(2)}) collective-permute-start(f32[5,34,1,256]{3,2,1,0:T(1,128)S(1)} %get-tuple-element.39), channel_id=1, source_target_pairs={{8,0},{16,8},{24,16},{9,1},{17,9},{25,17},{10,2},{18,10},{26,18},{... | collective-permute-start | bytes 522248 | tf_op jit(solution)/shard_map/ppermute | solution.py:27
  648.6 5.4 copy-start.17
  661.4 10.9 %collective-permute-start.41 = (f32[5,34,34,1]{2,3,1,0:T(1,128)}, f32[5,34,34,1]{2,3,1,0:T(1,128)}, u32[]{:S(2)}, u32[]{:S(2)}) collective-permute-start(f32[5,34,34,1]{2,3,1,0:T(1,128)} %copy.107), channel_id=1, source_target_pairs={{1,0},{2,1},{3,2},{4,3},{5,4},{6,5},{7,6},{9,8},{10,9},{11,10},{12... | collective-permute-start | bytes 69368 | tf_op jit(solution)/shard_map/ppermute | solution.py:27
  668.3 7.5 %collective-permute-start.40 = (f32[5,34,34,1]{2,3,1,0:T(1,128)}, f32[5,34,34,1]{2,3,1,0:T(1,128)}, u32[]{:S(2)}, u32[]{:S(2)}) collective-permute-start(f32[5,34,34,1]{2,3,1,0:T(1,128)} %copy.106), channel_id=1, source_target_pairs={{0,1},{1,2},{2,3},{3,4},{4,5},{5,6},{6,7},{8,9},{9,10},{10,11},{11... | collective-permute-start | bytes 69368 | tf_op jit(solution)/shard_map/ppermute | solution.py:24
  699.6 6.1 copy-start.2
  699.6 6.1 copy-start.11
  699.6 6.1 copy-start.12
  699.6 6.1 copy-start.13
  699.6 6.1 copy-start.18
  699.6 6.1 copy-start.20
  (3 other events, 5.3 us)
